TPU v7x, 256 devices: a whole 4x4x8 slice. The times are simulated.
256 devices in a mesh: strike: 64 (over y, z, core), dip: 4 (over x).
Axes of the slice: x: 4, y: 4, z: 8, core: 2. Of those that a mesh axis runs over, the one named last changes fastest.
Arguments:
- slip_rate: float32 [3, 4096, 1024], P(None, 'strike', 'dip'), may hold values from -6 to 6
- history: bfloat16 [4, 3, 2, 1024, 4096], P(None, None, None, ('strike', 'dip')), may hold values from -6 to 6
- lengths: int32 [1024, 4096], P(('strike', 'dip')), may hold values from 1 to 4, as said below
- prestress: float32 [2, 4096, 1024], P(None, 'strike', 'dip'), may hold values from -8 to 8
- normal_stress: float32 [4096, 1024], P('strike', 'dip'), may hold values from 8 to 16
- direct_effect: float32 [4096, 1024], P('strike', 'dip'), may hold values from 0.01 to 0.04
- state_log: float32 [4096, 1024], P('strike', 'dip'), may hold values from 1 to 5
Outputs:
- next_rates: float32 [3, 4096, 1024], P(None, 'strike', 'dip')
- next_state: float32 [4096, 1024], P('strike', 'dip')
Inputs may be any that keep to these rules, and one draw needn't show every extreme that they name: `lengths`: how many of the newest slip-rate spectra enter each wavenumber's stress transfer.
All inputs are finite; a program needn't handle non-finite values.
Results may differ from a plain program's by a relative error of at most 0.0003.
Values sent between devices are 32-bit elements; how exact they have to be, the bound alone decides.
No kernel may reach another device: no remote copies, remote signals or barrier semaphores. Data moves between devices by JAX's collectives and lax.ppermute only.
A program may use at most 128 MiB of HBM per device.

v0:
```python
import math
import jax
import jax.numpy as jnp
from jax import lax
from jax.sharding import PartitionSpec as P

HIST = 4
NEWTON = 2
time_step = 0.5
coupling = 0.5
decay_rate = 0.05
shear_speed = 0.6
opening_speed = 1.7
radiation = 0.5
healing = 1.0
slip_length = 2.0
highest = lax.Precision.HIGHEST


def area_sine(ratio):
    return jnp.log(ratio + jnp.sqrt(ratio * ratio + 1.0))


def wave_geometry(dip_modes, strike_modes, dip_cells, strike_cells):
    signed_dip = jnp.where(2 * dip_modes < dip_cells, dip_modes, dip_modes - dip_cells)
    signed_strike = jnp.where(
        2 * strike_modes < strike_cells, strike_modes, strike_modes - strike_cells
    )
    wave_dip = signed_dip.astype(jnp.float32) * (2.0 * math.pi / dip_cells)
    wave_strike = signed_strike.astype(jnp.float32) * (2.0 * math.pi / strike_cells)
    modulus = jnp.sqrt(wave_strike * wave_strike + wave_dip * wave_dip)
    anchor = (signed_dip == 0) & (signed_strike == 0)
    safe_modulus = jnp.where(anchor, 1.0, modulus)
    unit_strike = jnp.where(anchor, 1.0, wave_strike / safe_modulus)
    unit_dip = jnp.where(anchor, 0.0, wave_dip / safe_modulus)
    return (modulus, unit_strike, unit_dip)


def delay_mixing(geometry, delay):
    modulus, unit_strike, unit_dip = geometry
    phase_arg = modulus * (time_step * (delay + 1.0))
    envelope = -coupling * time_step * modulus * jnp.exp(-decay_rate * phase_arg)
    mode_two = envelope * jnp.cos(phase_arg)
    mode_three = envelope * jnp.cos(shear_speed * phase_arg)
    mode_one = envelope * jnp.cos(opening_speed * phase_arg)
    mix_along = unit_strike * unit_strike * mode_two + unit_dip * unit_dip * mode_three
    mix_cross = unit_strike * unit_dip * (mode_two - mode_three)
    mix_across = unit_dip * unit_dip * mode_two + unit_strike * unit_strike * mode_three
    return (mix_along, mix_cross, mix_across, mode_one)


def delay_term(spectrum, mixing, active):
    mix_along, mix_cross, mix_across, mode_one = mixing
    force_strike = (mix_along * spectrum[0] + mix_cross * spectrum[1]) * active
    force_dip = (mix_cross * spectrum[0] + mix_across * spectrum[1]) * active
    force_open = mode_one * spectrum[2] * active
    return jnp.stack([force_strike, force_dip, force_open])


def friction_step(force_field, prestress, normal_stress, direct_effect, state_log):
    load_strike = prestress[0] + force_field[0]
    load_dip = prestress[1] + force_field[1]
    traction = jnp.sqrt(load_strike * load_strike + load_dip * load_dip)
    strength = direct_effect * normal_stress
    factor = 2.0 * radiation * jnp.exp(-state_log)
    estimate = jnp.minimum(traction / strength, area_sine(traction / factor))
    for repeat in range(NEWTON):
        residual = traction - strength * estimate - factor * jnp.sinh(estimate)
        estimate = estimate + residual / (strength + factor * jnp.cosh(estimate))
    slip_speed = (traction - strength * estimate) / radiation
    unit_scale = slip_speed / jnp.maximum(traction, 1.0)
    new_rates = jnp.stack(
        [unit_scale * load_strike, unit_scale * load_dip, force_field[2] / radiation]
    )
    new_state = state_log + time_step * (healing * jnp.exp(-state_log) - slip_speed / slip_length)
    return (new_rates, new_state)


def phase_table(first_index, second_index, period):
    turn_count = first_index[:, None] * second_index[None, :] % period
    angle_table = turn_count.astype(jnp.float32) * (2.0 * math.pi / period)
    return (jnp.cos(angle_table), jnp.sin(angle_table))


def contract(pattern, first_operand, second_operand):
    return jnp.einsum(pattern, first_operand, second_operand, precision=highest)


def pair_section(part_real, part_imag, pattern, cos_table, sin_table, sign):
    out_real = contract(pattern, part_real, cos_table) - sign * contract(
        pattern, part_imag, sin_table
    )
    out_imag = contract(pattern, part_imag, cos_table) + sign * contract(
        pattern, part_real, sin_table
    )
    return (out_real, out_imag)


def twist_phase(part_real, part_imag, cos_table, sin_table, sign):
    out_real = cos_table * part_real - sign * sin_table * part_imag
    out_imag = cos_table * part_imag + sign * sin_table * part_real
    return (out_real, out_imag)


def shards(slip_rate, history, lengths, prestress, normal_stress, direct_effect, state_log):
    strike_count = lax.axis_size("strike")
    dip_count = lax.axis_size("dip")
    strike_index = lax.axis_index("strike")
    dip_index = lax.axis_index("dip")
    row_count = slip_rate.shape[1]
    dip_block = slip_rate.shape[2]
    mode_rows = history.shape[3]
    strike_cells = history.shape[4]
    dip_cells = dip_block * dip_count
    unit_modes = dip_count * mode_rows
    norm_dip = 1.0 / math.sqrt(dip_cells)
    norm_strike = 1.0 / math.sqrt(strike_cells)
    local_modes = jnp.arange(mode_rows, dtype=jnp.int32)
    dip_modes = (strike_index * dip_count + dip_index) * mode_rows + local_modes
    strike_modes = jnp.arange(strike_cells, dtype=jnp.int32)
    geometry = wave_geometry(dip_modes[:, None], strike_modes[None, :], dip_cells, strike_cells)
    coarse_all = jnp.arange(unit_modes, dtype=jnp.int32)
    coarse_own = dip_index * mode_rows + local_modes
    outer_index = jnp.arange(strike_count, dtype=jnp.int32)
    inner_index = jnp.arange(row_count, dtype=jnp.int32)
    cos_outer, sin_outer = phase_table(outer_index, outer_index, strike_count)
    cos_bend, sin_bend = phase_table(outer_index, inner_index, strike_cells)
    cos_bend = cos_bend * norm_strike
    sin_bend = sin_bend * norm_strike
    cos_inner, sin_inner = phase_table(inner_index, inner_index, row_count)

    def strike_forward(spectral):
        item_count = spectral.shape[0]
        grid_view = spectral.reshape(item_count, 2, mode_rows, strike_count, row_count)
        section_real, section_imag = pair_section(
            grid_view[:, 0], grid_view[:, 1], "ngpr,kp->ngkr", cos_outer, sin_outer, -1.0
        )
        bent_real, bent_imag = twist_phase(section_real, section_imag, cos_bend, sin_bend, -1.0)
        out_real, out_imag = pair_section(
            bent_real, bent_imag, "ngkr,rm->ngmk", cos_inner, sin_inner, -1.0
        )
        return jnp.stack([out_real, out_imag], axis=1).reshape(
            item_count, 2, mode_rows, strike_cells
        )

    def strike_inverse(spectral):
        grid_view = spectral.reshape(3, 2, mode_rows, row_count, strike_count)
        section_real, section_imag = pair_section(
            grid_view[:, 0], grid_view[:, 1], "ngmk,rm->ngrk", cos_inner, sin_inner, 1.0
        )
        bent_real, bent_imag = twist_phase(section_real, section_imag, cos_bend.T, sin_bend.T, 1.0)
        out_real, out_imag = pair_section(
            bent_real, bent_imag, "ngrk,kp->ngpr", cos_outer, sin_outer, 1.0
        )
        return jnp.stack([out_real, out_imag], axis=1).reshape(3, 2, mode_rows, strike_cells)

    def to_modes(space_field):
        gathered = lax.all_gather(space_field, "dip", axis=2, tiled=True)
        cos_first, sin_first = phase_table(coarse_all, coarse_own, unit_modes)
        cos_twist, sin_twist = phase_table(outer_index, coarse_own, dip_cells)
        grid_view = gathered.reshape(3, row_count, unit_modes, strike_count)
        first_real = contract("cxab,au->cxbu", grid_view, cos_first)
        first_imag = -contract("cxab,au->cxbu", grid_view, sin_first)
        bent_real, bent_imag = twist_phase(
            first_real, first_imag, cos_twist * norm_dip, sin_twist * norm_dip, -1.0
        )
        out_real, out_imag = pair_section(
            bent_real, bent_imag, "cxbi,bs->csix", cos_outer, sin_outer, -1.0
        )
        dip_spec = jnp.stack([out_real, out_imag], axis=1).reshape(3, 2, dip_block, row_count)
        return strike_forward(
            lax.all_to_all(dip_spec, "strike", split_axis=2, concat_axis=3, tiled=True)
        )

    def to_space(mode_field):
        mixed_rows = strike_inverse(mode_field)
        dip_spec = lax.all_to_all(mixed_rows, "strike", split_axis=3, concat_axis=2, tiled=True)
        gathered = lax.all_gather(dip_spec, "dip", axis=2, tiled=True)
        grid_view = gathered.reshape(3, 2, dip_count, strike_count, mode_rows, row_count)
        cos_last, sin_last = phase_table(coarse_own, coarse_all, unit_modes)
        first_real, first_imag = pair_section(
            grid_view[:, 0], grid_view[:, 1], "cdsix,bs->cxbdi", cos_outer, sin_outer, 1.0
        )
        first_real = first_real.reshape(3, row_count, strike_count, unit_modes)
        first_imag = first_imag.reshape(3, row_count, strike_count, unit_modes)
        cos_twist, sin_twist = phase_table(outer_index, coarse_all, dip_cells)
        bent_real, bent_imag = twist_phase(
            first_real, first_imag, cos_twist * norm_dip, sin_twist * norm_dip, 1.0
        )
        space_part = contract("cxbu,au->cxab", bent_real, cos_last) - contract(
            "cxbu,au->cxab", bent_imag, sin_last
        )
        return space_part.reshape(3, row_count, dip_block)

    def transfer(recent):
        recent_count = len(recent)
        summed = jnp.zeros(recent[0].shape, jnp.float32)
        for offset in range(HIST):
            if offset < recent_count:
                source = recent[offset]
            else:
                source = history[offset - recent_count].astype(jnp.float32)
            active = (offset < lengths).astype(jnp.float32)
            summed = summed + delay_term(source, delay_mixing(geometry, float(offset)), active)
        return summed

    first_spec = to_modes(slip_rate)
    force_field = to_space(transfer([first_spec]))
    next_rates, next_state = friction_step(
        force_field, prestress, normal_stress, direct_effect, state_log
    )
    second_spec = to_modes(next_rates)
    force_field = to_space(transfer([second_spec, first_spec]))
    next_rates, next_state = friction_step(
        force_field, prestress, normal_stress, direct_effect, next_state
    )
    return (next_rates, next_state)


def solution(mesh):
    return jax.shard_map(
        shards,
        mesh=mesh,
        in_specs=(
            P(None, "strike", "dip"),
            P(None, None, None, ("strike", "dip"), None),
            P(("strike", "dip"), None),
            P(None, "strike", "dip"),
            P("strike", "dip"),
            P("strike", "dip"),
            P("strike", "dip"),
        ),
        out_specs=(P(None, "strike", "dip"), P("strike", "dip")),
        check_vma=False,
    )
```

profile of v0, /device:TPU:1, one launch (start us, length us, event | category | flops | bytes accessed | tf_op | source)
XLA Modules:
  0.0 520.3 jit_solution(6019969516380714102)
XLA Ops:
  7.3 13.1 %all_gather.12 = f32[3,64,1024]{2,1,0:T(8,128)S(1)} all-gather(f32[3,64,256]{2,1,0:T(8,128)} %param.7), channel_id=1, replica_groups=mesh['strike'=64,'dip'=4] {'dip'}, dimensions={2}, use_global_device_ids=true | all-gather | bytes 983040 | tf_op jit(solution)/shard_map/all_gather | solution.py:158
  31.2 13.9 %all-to-all-start = ((f32[64,1,1536]{2,1,0:T(1,128)}), f32[64,1,1536]{2,1,0:T(1,128)S(1)}, u32[]{:S(2)}, u32[]{:S(2)}) async-start(f32[64,1,1536]{2,1,0:T(1,128)} %reshape.1792), calls=%async_computation | async-start | bytes 786432 | tf_op jit(solution)/shard_map/all_to_all | solution.py:172
  45.9 4.1 multiply_add_fusion.20
  60.7 2.8 multiply_add_fusion.5
  84.6 10.5 %copy.366 = f32[3,1,4,4096]{2,1,0,3:T(1,128)} copy(f32[3,1,4,4096]{3,2,0,1:T(4,128)S(1)} %stack.171) | data formatting | bytes 393216 | tf_op jit(solution)/shard_map/stack | solution.py:155
  96.7 10.3 %copy.367 = f32[3,1,4,4096]{2,1,0,3:T(1,128)} copy(f32[3,1,4,4096]{3,2,0,1:T(4,128)S(1)} %stack.172) | data formatting | bytes 393216 | tf_op jit(solution)/shard_map/stack | solution.py:155
  107.0 16.7 %fusion.506 = f32[4096,3,2,4]{3,2,1,0:T(2,128)} fusion(f32[3,1,4,4096]{2,1,0,3:T(1,128)} %copy.367, f32[3,1,4,4096]{2,1,0,3:T(1,128)} %copy.366), kind=kLoop, calls=%fused_computation.664 | loop fusion | flops 98304 | bytes 786432
  123.7 16.7 %reshape.1794 = f32[64,1,1536]{2,1,0:T(1,128)S(1)} reshape(f32[4096,3,2,4]{3,2,1,0:T(2,128)} %fusion.506) | data formatting | bytes 786432
  140.4 24.7 %all_to_all.66 = f32[64,1,1536]{2,1,0:T(1,128)S(1)} all-to-all(f32[64,1,1536]{2,1,0:T(1,128)S(1)} %reshape.1794), channel_id=1, replica_groups=mesh['strike'=64,'dip'=4] {'strike'}, dimensions={0} | all-to-all | bytes 786432 | tf_op jit(solution)/shard_map/all_to_all | solution.py:177
  166.7 21.1 %reshape.1795 = f32[4096,3,2,4]{3,2,1,0:T(2,128)} reshape(f32[64,1536]{1,0:T(8,128)S(1)} %reduce.1) | data formatting | bytes 786432
  187.8 16.1 %copy.455 = f32[3,2,4,64,64]{4,3,2,1,0:T(8,128)S(1)} copy(f32[3,2,4,64,64]{2,1,0,4,3:T(2,128)} %bitcast.476) | data formatting | bytes 786432 | tf_op jit(solution)/shard_map/all_to_all | solution.py:177
  205.5 38.9 %all-gather.3.cloned.1.call-done = f32[3,2,1024,64]{3,2,1,0:T(8,128)} async-done(((f32[3,2,256,64]{3,2,1,0:T(8,128)}), f32[3,2,1024,64]{3,2,1,0:T(8,128)}) %all-gather.3.cloned.1.call-update) | async-done | bytes 1572880 | tf_op jit(solution)/shard_map/all_gather | solution.py:178
  244.4 2.1 fusion.502
  248.2 2.8 fusion.16
  251.0 2.8 convolution_add_fusion.1
  255.9 4.2 convolution_subtract_fusion.1
  267.3 10.6 %all_gather.14 = f32[3,64,1024]{2,1,0:T(8,128)S(1)} all-gather(f32[3,64,256]{2,1,0:T(8,128)S(1)} %pad_maximum_fusion.6), channel_id=1, replica_groups=mesh['strike'=64,'dip'=4] {'dip'}, dimensions={2}, use_global_device_ids=true | all-gather | bytes 983040 | tf_op jit(solution)/shard_map/all_gather | solution.py:158
  288.9 14.7 %all-to-all-start.2 = ((f32[64,1,1536]{2,1,0:T(1,128)}), f32[64,1,1536]{2,1,0:T(1,128)S(1)}, u32[]{:S(2)}, u32[]{:S(2)}) async-start(f32[64,1,1536]{2,1,0:T(1,128)} %reshape.1796), calls=%async_computation.2 | async-start | bytes 786432 | tf_op jit(solution)/shard_map/all_to_all | solution.py:172
  307.8 10.3 %all-to-all-done.2 = f32[64,1,1536]{2,1,0:T(1,128)S(1)} async-done(((f32[64,1,1536]{2,1,0:T(1,128)}), f32[64,1,1536]{2,1,0:T(1,128)S(1)}, u32[]{:S(2)}, u32[]{:S(2)}) %all-to-all-start.2) | async-done | bytes 393248 | tf_op jit(solution)/shard_map/all_to_all | solution.py:172
  336.6 10.3 %copy.396 = f32[3,1,4,4096]{2,1,0,3:T(1,128)} copy(f32[3,1,4,4096]{3,2,0,1:T(4,128)S(1)} %stack.193) | data formatting | bytes 393216 | tf_op jit(solution)/shard_map/stack | solution.py:155
  348.6 10.3 %copy.397 = f32[3,1,4,4096]{2,1,0,3:T(1,128)} copy(f32[3,1,4,4096]{3,2,0,1:T(4,128)S(1)} %stack.194) | data formatting | bytes 393216 | tf_op jit(solution)/shard_map/stack | solution.py:155
  358.8 16.7 %fusion.505 = f32[4096,3,2,4]{3,2,1,0:T(2,128)} fusion(f32[3,1,4,4096]{2,1,0,3:T(1,128)} %copy.397, f32[3,1,4,4096]{2,1,0,3:T(1,128)} %copy.396), kind=kLoop, calls=%fused_computation.663 | loop fusion | flops 98304 | bytes 786432
  375.5 16.7 %reshape.1798 = f32[64,1,1536]{2,1,0:T(1,128)S(1)} reshape(f32[4096,3,2,4]{3,2,1,0:T(2,128)} %fusion.505) | data formatting | bytes 786432
  392.3 20.6 %all_to_all.67 = f32[64,1,1536]{2,1,0:T(1,128)S(1)} all-to-all(f32[64,1,1536]{2,1,0:T(1,128)S(1)} %reshape.1798), channel_id=1, replica_groups=mesh['strike'=64,'dip'=4] {'strike'}, dimensions={0} | all-to-all | bytes 786432 | tf_op jit(solution)/shard_map/all_to_all | solution.py:177
  414.4 21.1 %reshape.1799 = f32[4096,3,2,4]{3,2,1,0:T(2,128)} reshape(f32[64,1536]{1,0:T(8,128)S(1)} %reduce.3) | data formatting | bytes 786432
  435.5 15.9 %copy.467 = f32[3,2,4,64,64]{4,3,2,1,0:T(8,128)S(1)} copy(f32[3,2,4,64,64]{2,1,0,4,3:T(2,128)} %bitcast.477) | data formatting | bytes 786432 | tf_op jit(solution)/shard_map/all_to_all | solution.py:177
  452.9 37.3 %all-gather.5.cloned.1.call-done = f32[3,2,1024,64]{3,2,1,0:T(8,128)} async-done(((f32[3,2,256,64]{3,2,1,0:T(8,128)}), f32[3,2,1024,64]{3,2,1,0:T(8,128)}) %all-gather.5.cloned.1.call-update) | async-done | bytes 1572880 | tf_op jit(solution)/shard_map/all_gather | solution.py:178
  490.2 2.1 fusion.501
  494.0 2.8 fusion.18
  496.8 2.8 convolution_add_fusion
  499.6 2.1 copy.403
  501.7 4.2 convolution_subtract_fusion
  (207 shorter events, 105.6 us)
Async XLA Ops:
  28.9 16.8 %copy-start.34 = (s32[4,4096]{1,0:T(4,128)S(1)}, s32[4,4096]{1,0:T(4,128)}, u32[]{:S(2)}) copy-start(s32[4,4096]{1,0:T(4,128)} %param.9) | copy-start | bytes 196612
  28.9 16.8 %copy-start.33 = (bf16[4,3,2,4,4096]{4,3,2,1,0:T(4,128)(2,1)S(1)}, bf16[4,3,2,4,4096]{4,3,2,1,0:T(4,128)(2,1)}, u32[]{:S(2)}) copy-start(bf16[4,3,2,4,4096]{4,3,2,1,0:T(4,128)(2,1)} %param.8) | copy-start | bytes 2359300
  31.2 32.3 %all-to-all-start = ((f32[64,1,1536]{2,1,0:T(1,128)}), f32[64,1,1536]{2,1,0:T(1,128)S(1)}, u32[]{:S(2)}, u32[]{:S(2)}) async-start(f32[64,1,1536]{2,1,0:T(1,128)} %reshape.1792), calls=%async_computation | async-start | bytes 786432 | tf_op jit(solution)/shard_map/all_to_all | solution.py:172
  45.1 199.3 %all-gather.3.cloned.1.call-start = ((), (), s32[]{:S(2)}) async-start(), calls=%async_computation.4 | async-start | bytes 3932160 | tf_op jit(solution)/shard_map/all_gather | solution.py:178
  63.5 11.3 %copy-start.7 = (f32[4,64,64]{2,1,0:T(8,128)}, f32[4,64,64]{2,1,0:T(8,128)S(1)}, u32[]{:S(2)}) copy-start(f32[4,64,64]{2,1,0:T(8,128)S(1)} %get-tuple-element.73) | copy-start | bytes 196612
  63.5 12.3 %copy-start.1 = (f32[4,64,64]{2,1,0:T(8,128)}, f32[4,64,64]{2,1,0:T(8,128)S(1)}, u32[]{:S(2)}) copy-start(f32[4,64,64]{2,1,0:T(8,128)S(1)} %get-tuple-element.55) | copy-start | bytes 196612
  63.5 12.3 %copy-start.3 = (f32[4,64,64]{2,1,0:T(8,128)}, f32[4,64,64]{2,1,0:T(8,128)S(1)}, u32[]{:S(2)}) copy-start(f32[4,64,64]{2,1,0:T(8,128)S(1)} %get-tuple-element.56) | copy-start | bytes 196612
  63.5 12.3 %copy-start.5 = (f32[4,64,64]{2,1,0:T(8,128)}, f32[4,64,64]{2,1,0:T(8,128)S(1)}, u32[]{:S(2)}) copy-start(f32[4,64,64]{2,1,0:T(8,128)S(1)} %get-tuple-element.58) | copy-start | bytes 196612
  74.8 1.9 copy-start.18
  75.8 1.5 copy-start.16
  75.8 1.6 copy-start.17
  263.4 1.4 copy-start
  286.6 17.2 %copy-start.29 = (f32[1,2,4,4096]{3,2,1,0:T(4,128)S(1)}, f32[1,2,4,4096]{3,2,1,0:T(4,128)}, u32[]{:S(2)}) copy-start(f32[1,2,4,4096]{3,2,1,0:T(4,128)} %get-tuple-element.48) | copy-start | bytes 393220
  287.3 16.8 %copy-start.28 = (f32[1,2,4,4096]{3,2,1,0:T(4,128)S(1)}, f32[1,2,4,4096]{3,2,1,0:T(4,128)}, u32[]{:S(2)}) copy-start(f32[1,2,4,4096]{3,2,1,0:T(4,128)} %get-tuple-element.47) | copy-start | bytes 393220
  287.3 16.9 %copy-start.27 = (f32[1,2,4,4096]{3,2,1,0:T(4,128)S(1)}, f32[1,2,4,4096]{3,2,1,0:T(4,128)}, u32[]{:S(2)}) copy-start(f32[1,2,4,4096]{3,2,1,0:T(4,128)} %get-tuple-element.46) | copy-start | bytes 393220
  287.3 17.9 %copy-start.32 = (f32[1,2,4,4096]{3,2,1,0:T(4,128)S(1)}, f32[1,2,4,4096]{3,2,1,0:T(4,128)}, u32[]{:S(2)}) copy-start(f32[1,2,4,4096]{3,2,1,0:T(4,128)} %get-tuple-element.51) | copy-start | bytes 393220
  287.3 18.7 %copy-start.31 = (f32[1,2,4,4096]{3,2,1,0:T(4,128)S(1)}, f32[1,2,4,4096]{3,2,1,0:T(4,128)}, u32[]{:S(2)}) copy-start(f32[1,2,4,4096]{3,2,1,0:T(4,128)} %get-tuple-element.50) | copy-start | bytes 393220
  288.9 18.0 %copy-start.30 = (f32[1,2,4,4096]{3,2,1,0:T(4,128)S(1)}, f32[1,2,4,4096]{3,2,1,0:T(4,128)}, u32[]{:S(2)}) copy-start(f32[1,2,4,4096]{3,2,1,0:T(4,128)} %get-tuple-element.49) | copy-start | bytes 393220
  288.9 29.2 %all-to-all-start.2 = ((f32[64,1,1536]{2,1,0:T(1,128)}), f32[64,1,1536]{2,1,0:T(1,128)S(1)}, u32[]{:S(2)}, u32[]{:S(2)}) async-start(f32[64,1,1536]{2,1,0:T(1,128)} %reshape.1796), calls=%async_computation.2 | async-start | bytes 786432 | tf_op jit(solution)/shard_map/all_to_all | solution.py:172
  303.6 186.7 %all-gather.5.cloned.1.call-start = ((), (), s32[]{:S(2)}) async-start(), calls=%async_computation.5 | async-start | bytes 3932160 | tf_op jit(solution)/shard_map/all_gather | solution.py:178
  325.7 2.9 copy-start.2
  325.7 2.9 copy-start.4
  325.7 2.9 copy-start.6
  325.7 2.9 copy-start.8
  327.2 1.7 copy-start.9
  327.2 1.7 copy-start.19
  327.2 1.7 copy-start.20
  327.2 1.7 copy-start.21
  327.2 1.7 copy-start.22
  327.2 1.7 copy-start.23
  327.2 1.7 copy-start.24
  509.2 1.4 copy-start.26
  (7 other events, 7.7 us)
Sparse Core Ops, SparseCore 0:
  205.5 38.8 all-gather.2
  453.0 37.1 all-gather.4
where the time goes:
time: 528 us; the launch traced here: 520 us
  local copies, waits for them, and re-layouts  189 us (36%)
  waiting for transfers between devices  86.6 us (16%)
  matrix products  75.4 us (14%)
  blocking collectives  69 us (13%)
  other arithmetic  56.3 us (11%)
  starting transfers between devices  29.3 us (6%)
  between operations  15.2 us (3%)
    unnamed x78, local copies, waits for them, and re-layouts  81.5 us
    all_gather x2, waiting for transfers between devices, to_space(): gathered = lax.all_gather(dip_spec, 'dip', axis=2, tiled=True)  76.3 us
    dot_general x56, matrix products, contract(): return jnp.einsum(pattern, first_operand, second_operand, precision=highest)  75.4 us
    all_to_all x2, blocking collectives, to_space(): lax.all_to_all(mixed_rows, 'strike', split_axis=3, concat_axis=2, tiled=T...  45.3 us
    another operation x8, local copies, waits for them, and re-layouts, strike_inverse(): jnp.stack([out_real, out_imag], axis=1)  42.1 us
    all_to_all x4, local copies, waits for them, and re-layouts, to_space(): lax.all_to_all(mixed_rows, 'strike', split_axis=3, concat_axis=2, tiled=T...  34.9 us
    unnamed x2, other arithmetic  33.4 us
    all_to_all x2, starting transfers between devices, to_modes(): lax.all_to_all(dip_spec, 'strike', split_axis=2, concat_axis=3, tiled=True)  28.6 us
  transfers between devices with their start and end apart: 4, of which 3 were waited for; matrix products, arithmetic and copies ran while one was open for 4% of the time, Pallas kernels for 0%

commit v1 on v0

--- a/solution.py
+++ b/solution.py
@@ -15,6 +15,11 @@
 healing = 1.0
 slip_length = 2.0
 highest = lax.Precision.HIGHEST
+
+
+def gather_from_all(shard, axis, dim):
+    copies = jnp.concatenate([shard] * lax.axis_size(axis), axis=dim)
+    return lax.all_to_all(copies, axis, dim, dim, tiled=True)
 
 
 def area_sine(ratio):
@@ -175,7 +180,7 @@
     def to_space(mode_field):
         mixed_rows = strike_inverse(mode_field)
         dip_spec = lax.all_to_all(mixed_rows, "strike", split_axis=3, concat_axis=2, tiled=True)
-        gathered = lax.all_gather(dip_spec, "dip", axis=2, tiled=True)
+        gathered = gather_from_all(dip_spec, "dip", 2)
         grid_view = gathered.reshape(3, 2, dip_count, strike_count, mode_rows, row_count)
         cos_last, sin_last = phase_table(coarse_own, coarse_all, unit_modes)
         first_real, first_imag = pair_section(

time: 528 us -> 513 us (0.972)
  waiting for transfers between devices: 86.6 us -> 30.3 us
  blocking collectives: 69 us -> 94.7 us
  local copies, waits for them, and re-layouts: 189 us -> 204 us
  between operations: 15.2 us -> 1.96 us
  other arithmetic: 56.3 us -> 69.3 us
    all_gather x2 -> x0, waiting for transfers between devices: 76.3 us -> none  [to_space(): gathered = lax.all_gather(dip_spec, 'dip', axis=2, tiled=True)]
    all_to_all x0 -> x1, blocking collectives: none -> 23.9 us  [gather_from_all(): return lax.all_to_all(copies, axis, dim, dim, tiled=True)]
    all_to_all x0 -> x1, waiting for transfers between devices: none -> 19.9 us  [gather_from_all(): return lax.all_to_all(copies, axis, dim, dim, tiled=True)]
    unnamed x78 -> x82, local copies, waits for them, and re-layouts: 81.5 us -> 97.4 us
    all_to_all x0 -> x2, other arithmetic: none -> 12.6 us  [gather_from_all(): return lax.all_to_all(copies, axis, dim, dim, tiled=True)]
  transfers between devices with their start and end apart: 4 -> 3, of which waited for: 3 -> 2; matrix products, arithmetic and copies ran while one was open for 4% -> 4% of each run, Pallas kernels for 0% -> 0%
where the time goes in v1:
time: 513 us; the launch traced here: 504 us
  local copies, waits for them, and re-layouts  204 us (40%)
  blocking collectives  94.7 us (18%)
  matrix products  75.8 us (15%)
  other arithmetic  69.3 us (14%)
  waiting for transfers between devices  30.3 us (6%)
  starting transfers between devices  28.7 us (6%)
    unnamed x82, local copies, waits for them, and re-layouts  97.4 us
    dot_general x56, matrix products, contract(): return jnp.einsum(pattern, first_operand, second_operand, precision=highest)  75.8 us
    all_to_all x2, blocking collectives, to_space(): lax.all_to_all(mixed_rows, 'strike', split_axis=3, concat_axis=2, tiled=T...  45.9 us
    another operation x8, local copies, waits for them, and re-layouts, strike_inverse(): jnp.stack([out_real, out_imag], axis=1)  42.4 us
    unnamed x2, other arithmetic  33.5 us
    all_to_all x4, local copies, waits for them, and re-layouts, to_space(): lax.all_to_all(mixed_rows, 'strike', split_axis=3, concat_axis=2, tiled=T...  32.5 us
    all_gather x2, blocking collectives, to_modes(): gathered = lax.all_gather(space_field, 'dip', axis=2, tiled=True)  24.9 us
    all_to_all x2, starting transfers between devices, to_modes(): lax.all_to_all(dip_spec, 'strike', split_axis=2, concat_axis=3, tiled=True)  24.4 us
  transfers between devices with their start and end apart: 3, of which 2 were waited for; matrix products, arithmetic and copies ran while one was open for 4% of the time, Pallas kernels for 0%

profile of v1, /device:TPU:1, one launch (start us, length us, event | category | flops | bytes accessed | tf_op | source)
XLA Modules:
  0.0 504.4 jit_solution(6167115436566713718)
XLA Ops:
  0.8 13.1 %all_gather.6 = f32[3,64,1024]{2,1,0:T(8,128)S(1)} all-gather(f32[3,64,256]{2,1,0:T(8,128)} %param.7), channel_id=1, replica_groups=mesh['strike'=64,'dip'=4] {'dip'}, dimensions={2}, use_global_device_ids=true | all-gather | bytes 983040 | tf_op jit(solution)/shard_map/all_gather | solution.py:163
  24.6 14.1 %all-to-all-start = ((f32[64,1,1536]{2,1,0:T(1,128)}), f32[64,1,1536]{2,1,0:T(1,128)S(1)}, u32[]{:S(2)}, u32[]{:S(2)}) async-start(f32[64,1,1536]{2,1,0:T(1,128)} %reshape.1792), calls=%async_computation | async-start | bytes 786432 | tf_op jit(solution)/shard_map/all_to_all | solution.py:177
  39.0 4.1 multiply_add_fusion.20
  77.6 10.8 %copy.378 = f32[3,1,4,4096]{2,1,0,3:T(1,128)} copy(f32[3,1,4,4096]{3,2,0,1:T(4,128)S(1)} %stack.171) | data formatting | bytes 393216 | tf_op jit(solution)/shard_map/stack | solution.py:160
  89.9 10.3 %copy.379 = f32[3,1,4,4096]{2,1,0,3:T(1,128)} copy(f32[3,1,4,4096]{3,2,0,1:T(4,128)S(1)} %stack.172) | data formatting | bytes 393216 | tf_op jit(solution)/shard_map/stack | solution.py:160
  100.2 16.7 %fusion.506 = f32[4096,3,2,4]{3,2,1,0:T(2,128)} fusion(f32[3,1,4,4096]{2,1,0,3:T(1,128)} %copy.379, f32[3,1,4,4096]{2,1,0,3:T(1,128)} %copy.378), kind=kLoop, calls=%fused_computation.666 | loop fusion | flops 98304 | bytes 786432
  116.9 16.7 %reshape.1794 = f32[64,1,1536]{2,1,0:T(1,128)S(1)} reshape(f32[4096,3,2,4]{3,2,1,0:T(2,128)} %fusion.506) | data formatting | bytes 786432
  133.7 24.9 %all_to_all.76 = f32[64,1,1536]{2,1,0:T(1,128)S(1)} all-to-all(f32[64,1,1536]{2,1,0:T(1,128)S(1)} %reshape.1794), channel_id=1, replica_groups=mesh['strike'=64,'dip'=4] {'strike'}, dimensions={0} | all-to-all | bytes 786432 | tf_op jit(solution)/shard_map/all_to_all | solution.py:182
  160.1 21.1 %reshape.1795 = f32[4096,3,2,4]{3,2,1,0:T(2,128)} reshape(f32[64,1536]{1,0:T(8,128)S(1)} %reduce.1) | data formatting | bytes 786432
  181.2 15.7 %copy.471 = f32[3,2,4,64,64]{4,3,2,1,0:T(8,128)S(1)} copy(f32[3,2,4,64,64]{2,1,0,4,3:T(2,128)} %bitcast.484) | data formatting | bytes 786432 | tf_op jit(solution)/shard_map/all_to_all | solution.py:182
  200.1 4.1 reshape.1796
  204.2 4.3 all-to-all-start.2
  208.6 19.9 %all-to-all-done.2 = f32[4,1,98304]{2,1,0:T(1,128)S(1)} async-done(((f32[4,1,98304]{2,1,0:T(1,128)}), f32[4,1,98304]{2,1,0:T(1,128)S(1)}, u32[]{:S(2)}, u32[]{:S(2)}) %all-to-all-start.2) | async-done | bytes 1572896 | tf_op jit(solution)/shard_map/all_to_all | solution.py:22
  228.5 6.3 %reduce.2 = f32[4,98304]{1,0:T(4,128)} reduce(f32[4,1,98304]{2,1,0:T(1,128)S(1)} %all-to-all-done.2, f32[]{:T(128)} %broadcast.2493), dimensions={1}, to_apply=%all_to_all.61.reduce_sub_computation | reduce | bytes 3145732 | tf_op jit(solution)/shard_map/all_to_all | solution.py:22
  234.8 3.9 reshape.1797
  243.6 3.1 convolution_add_fusion.1
  248.8 4.2 convolution_subtract_fusion.1
  260.2 11.8 %all_gather.7 = f32[3,64,1024]{2,1,0:T(8,128)S(1)} all-gather(f32[3,64,256]{2,1,0:T(8,128)S(1)} %pad_maximum_fusion.8), channel_id=1, replica_groups=mesh['strike'=64,'dip'=4] {'dip'}, dimensions={2}, use_global_device_ids=true | all-gather | bytes 983040 | tf_op jit(solution)/shard_map/all_gather | solution.py:163
  283.0 10.3 %all-to-all-start.3 = ((f32[64,1,1536]{2,1,0:T(1,128)}), f32[64,1,1536]{2,1,0:T(1,128)S(1)}, u32[]{:S(2)}, u32[]{:S(2)}) async-start(f32[64,1,1536]{2,1,0:T(1,128)} %reshape.1798), calls=%async_computation.3 | async-start | bytes 786432 | tf_op jit(solution)/shard_map/all_to_all | solution.py:177
  297.3 10.4 %all-to-all-done.3 = f32[64,1,1536]{2,1,0:T(1,128)S(1)} async-done(((f32[64,1,1536]{2,1,0:T(1,128)}), f32[64,1,1536]{2,1,0:T(1,128)S(1)}, u32[]{:S(2)}, u32[]{:S(2)}) %all-to-all-start.3) | async-done | bytes 393248 | tf_op jit(solution)/shard_map/all_to_all | solution.py:177
  326.0 10.4 %copy.410 = f32[3,1,4,4096]{2,1,0,3:T(1,128)} copy(f32[3,1,4,4096]{3,2,0,1:T(4,128)S(1)} %stack.193) | data formatting | bytes 393216 | tf_op jit(solution)/shard_map/stack | solution.py:160
  338.0 10.3 %copy.411 = f32[3,1,4,4096]{2,1,0,3:T(1,128)} copy(f32[3,1,4,4096]{3,2,0,1:T(4,128)S(1)} %stack.194) | data formatting | bytes 393216 | tf_op jit(solution)/shard_map/stack | solution.py:160
  348.2 16.7 %fusion.505 = f32[4096,3,2,4]{3,2,1,0:T(2,128)} fusion(f32[3,1,4,4096]{2,1,0,3:T(1,128)} %copy.411, f32[3,1,4,4096]{2,1,0,3:T(1,128)} %copy.410), kind=kLoop, calls=%fused_computation.665 | loop fusion | flops 98304 | bytes 786432
  365.0 16.7 %reshape.1800 = f32[64,1,1536]{2,1,0:T(1,128)S(1)} reshape(f32[4096,3,2,4]{3,2,1,0:T(2,128)} %fusion.505) | data formatting | bytes 786432
  381.7 21.0 %all_to_all.77 = f32[64,1,1536]{2,1,0:T(1,128)S(1)} all-to-all(f32[64,1,1536]{2,1,0:T(1,128)S(1)} %reshape.1800), channel_id=1, replica_groups=mesh['strike'=64,'dip'=4] {'strike'}, dimensions={0} | all-to-all | bytes 786432 | tf_op jit(solution)/shard_map/all_to_all | solution.py:182
  404.2 21.1 %reshape.1801 = f32[4096,3,2,4]{3,2,1,0:T(2,128)} reshape(f32[64,1536]{1,0:T(8,128)S(1)} %reduce.4) | data formatting | bytes 786432
  425.3 15.7 %copy.483 = f32[3,2,4,64,64]{4,3,2,1,0:T(8,128)S(1)} copy(f32[3,2,4,64,64]{2,1,0,4,3:T(2,128)} %bitcast.485) | data formatting | bytes 786432 | tf_op jit(solution)/shard_map/all_to_all | solution.py:182
  444.3 4.1 reshape.1802
  448.4 23.9 %all_to_all.78 = f32[4,1,98304]{2,1,0:T(1,128)S(1)} all-to-all(f32[4,1,98304]{2,1,0:T(1,128)} %reshape.1802), channel_id=1, replica_groups=mesh['strike'=64,'dip'=4] {'dip'}, dimensions={0} | all-to-all | bytes 3145728 | tf_op jit(solution)/shard_map/all_to_all | solution.py:22
  472.3 6.3 %reduce.5 = f32[4,98304]{1,0:T(4,128)} reduce(f32[4,1,98304]{2,1,0:T(1,128)S(1)} %all_to_all.78, f32[]{:T(128)} %broadcast.2493), dimensions={1}, to_apply=%all_to_all.69.reduce_sub_computation | reduce | bytes 3145732 | tf_op jit(solution)/shard_map/all_to_all | solution.py:22
  478.6 3.9 reshape.1803
  492.6 4.2 convolution_subtract_fusion
  (216 shorter events, 122.0 us)
Async XLA Ops:
  22.4 16.4 %copy-start.34 = (s32[4,4096]{1,0:T(4,128)S(1)}, s32[4,4096]{1,0:T(4,128)}, u32[]{:S(2)}) copy-start(s32[4,4096]{1,0:T(4,128)} %param.9) | copy-start | bytes 196612
  22.4 16.5 %copy-start.33 = (bf16[4,3,2,4,4096]{4,3,2,1,0:T(4,128)(2,1)S(1)}, bf16[4,3,2,4,4096]{4,3,2,1,0:T(4,128)(2,1)}, u32[]{:S(2)}) copy-start(bf16[4,3,2,4,4096]{4,3,2,1,0:T(4,128)(2,1)} %param.8) | copy-start | bytes 2359300
  24.6 31.9 %all-to-all-start = ((f32[64,1,1536]{2,1,0:T(1,128)}), f32[64,1,1536]{2,1,0:T(1,128)S(1)}, u32[]{:S(2)}, u32[]{:S(2)}) async-start(f32[64,1,1536]{2,1,0:T(1,128)} %reshape.1792), calls=%async_computation | async-start | bytes 786432 | tf_op jit(solution)/shard_map/all_to_all | solution.py:177
  56.5 11.2 %copy-start.7 = (f32[4,64,64]{2,1,0:T(8,128)}, f32[4,64,64]{2,1,0:T(8,128)S(1)}, u32[]{:S(2)}) copy-start(f32[4,64,64]{2,1,0:T(8,128)S(1)} %get-tuple-element.73) | copy-start | bytes 196612
  56.5 12.3 %copy-start.1 = (f32[4,64,64]{2,1,0:T(8,128)}, f32[4,64,64]{2,1,0:T(8,128)S(1)}, u32[]{:S(2)}) copy-start(f32[4,64,64]{2,1,0:T(8,128)S(1)} %get-tuple-element.55) | copy-start | bytes 196612
  56.5 12.3 %copy-start.3 = (f32[4,64,64]{2,1,0:T(8,128)}, f32[4,64,64]{2,1,0:T(8,128)S(1)}, u32[]{:S(2)}) copy-start(f32[4,64,64]{2,1,0:T(8,128)S(1)} %get-tuple-element.56) | copy-start | bytes 196612
  56.5 12.3 %copy-start.5 = (f32[4,64,64]{2,1,0:T(8,128)}, f32[4,64,64]{2,1,0:T(8,128)S(1)}, u32[]{:S(2)}) copy-start(f32[4,64,64]{2,1,0:T(8,128)S(1)} %get-tuple-element.58) | copy-start | bytes 196612
  67.7 2.0 copy-start.18
  68.7 1.4 copy-start.15
  68.7 1.5 copy-start.16
  68.8 1.6 copy-start.17
  204.2 24.3 %all-to-all-start.2 = ((f32[4,1,98304]{2,1,0:T(1,128)}), f32[4,1,98304]{2,1,0:T(1,128)S(1)}, u32[]{:S(2)}, u32[]{:S(2)}) async-start(f32[4,1,98304]{2,1,0:T(1,128)} %reshape.1796), calls=%async_computation.2 | async-start | bytes 3145728 | tf_op jit(solution)/shard_map/all_to_all | solution.py:22
  256.3 1.4 copy-start
  280.8 12.6 %copy-start.29 = (f32[1,2,4,4096]{3,2,1,0:T(4,128)S(1)}, f32[1,2,4,4096]{3,2,1,0:T(4,128)}, u32[]{:S(2)}) copy-start(f32[1,2,4,4096]{3,2,1,0:T(4,128)} %get-tuple-element.48) | copy-start | bytes 393220
  281.4 12.2 %copy-start.28 = (f32[1,2,4,4096]{3,2,1,0:T(4,128)S(1)}, f32[1,2,4,4096]{3,2,1,0:T(4,128)}, u32[]{:S(2)}) copy-start(f32[1,2,4,4096]{3,2,1,0:T(4,128)} %get-tuple-element.47) | copy-start | bytes 393220
  281.4 12.4 %copy-start.27 = (f32[1,2,4,4096]{3,2,1,0:T(4,128)S(1)}, f32[1,2,4,4096]{3,2,1,0:T(4,128)}, u32[]{:S(2)}) copy-start(f32[1,2,4,4096]{3,2,1,0:T(4,128)} %get-tuple-element.46) | copy-start | bytes 393220
  281.4 13.2 %copy-start.32 = (f32[1,2,4,4096]{3,2,1,0:T(4,128)S(1)}, f32[1,2,4,4096]{3,2,1,0:T(4,128)}, u32[]{:S(2)}) copy-start(f32[1,2,4,4096]{3,2,1,0:T(4,128)} %get-tuple-element.51) | copy-start | bytes 393220
  281.4 14.1 %copy-start.31 = (f32[1,2,4,4096]{3,2,1,0:T(4,128)S(1)}, f32[1,2,4,4096]{3,2,1,0:T(4,128)}, u32[]{:S(2)}) copy-start(f32[1,2,4,4096]{3,2,1,0:T(4,128)} %get-tuple-element.50) | copy-start | bytes 393220
  283.0 13.4 %copy-start.30 = (f32[1,2,4,4096]{3,2,1,0:T(4,128)S(1)}, f32[1,2,4,4096]{3,2,1,0:T(4,128)}, u32[]{:S(2)}) copy-start(f32[1,2,4,4096]{3,2,1,0:T(4,128)} %get-tuple-element.49) | copy-start | bytes 393220
  283.0 24.7 %all-to-all-start.3 = ((f32[64,1,1536]{2,1,0:T(1,128)}), f32[64,1,1536]{2,1,0:T(1,128)S(1)}, u32[]{:S(2)}, u32[]{:S(2)}) async-start(f32[64,1,1536]{2,1,0:T(1,128)} %reshape.1798), calls=%async_computation.3 | async-start | bytes 786432 | tf_op jit(solution)/shard_map/all_to_all | solution.py:177
  315.3 2.9 copy-start.2
  315.3 2.9 copy-start.4
  315.3 2.9 copy-start.6
  315.3 2.9 copy-start.8
  316.8 1.7 copy-start.9
  316.8 1.7 copy-start.19
  316.8 1.7 copy-start.20
  316.8 1.7 copy-start.21
  316.8 1.7 copy-start.22
  316.8 1.7 copy-start.23
  316.8 1.7 copy-start.24
  500.1 1.4 copy-start.26
  (6 other events, 6.3 us)
